TPU v7x, 256 devices: a whole 4x4x8 slice. The times are simulated.
256 devices in a mesh: dp: 8 (over z_lo, core), seq: 16 (over x, y), mp: 2 (over z_hi).
Axes of the slice: x: 4, y: 4, z: 8 (z_hi: 2, z_lo: 4; z = z_hi * 4 + z_lo), core: 2. Of those that a mesh axis runs over, the one named last changes fastest.
Arguments:
- features: bfloat16 [8, 8192, 1408], P('dp', ('seq', 'mp')), may hold values from -6 to 6
- conv_weight: bfloat16 [5, 1408, 1536], P(None, ('seq', 'mp')), may hold values from -0.0625 to 0.0625
- norm_gain: float32 [1536], replicated, may hold values from 0.25 to 1.75
- query_weight: bfloat16 [1536, 1024], replicated, may hold values from -0.15625 to 0.15625
- keyval_weight: bfloat16 [1536, 320], replicated, may hold values from -0.15625 to 0.15625
- head_scale: float32 [8], replicated, may hold values from 0.5 to 24
- output_weight: bfloat16 [1536, 1536], replicated, may hold values from -0.15625 to 0.15625
- pair_weight: bfloat16 [1536, 256], replicated, may hold values from -0.625 to 0.625
- pair_input: bfloat16 [8, 256, 256, 128], P('dp', ('seq', 'mp')), may hold values from -6 to 6
- flip_weight: bfloat16 [128, 128], replicated, may hold values from -0.5 to 0.5
- pair_cotangent: bfloat16 [8, 256, 256, 128], P('dp', ('seq', 'mp')), may hold values from -0.0234375 to 0.0234375
Outputs:
- block_out: bfloat16 [8, 4096, 1536], P('dp', ('seq', 'mp'))
- pair_out: bfloat16 [8, 256, 256, 128], P('dp', ('seq', 'mp'))
- grad_flip: float32 [128, 128], replicated
All inputs are finite; a program needn't handle non-finite values.
Results may differ from a plain program's by a relative error of at most 0.011.
Values may be sent and summed in bfloat16 or wider, within the bound.
A program may use at most 192 MiB of HBM per device.

v0:
```python
import math
import jax
import jax.numpy as jnp
from jax import lax
from jax.sharding import PartitionSpec as P

PAIR_POOL = 16
norm_eps = 1e-06
logit_cap = 50.0


def padded_2(shard, sides, width):
    for axis, dim in sides:
        devices, length = (lax.axis_size(axis), shard.shape[dim])
        up = [(i, (i + 1) % devices) for i in range(devices - 1)]
        down = [(j, i) for i, j in up]
        last = lax.slice_in_dim(shard, length - width, length, axis=dim)
        initial = lax.slice_in_dim(shard, 0, width, axis=dim)
        before = lax.ppermute(last, axis, up)
        after = lax.ppermute(initial, axis, down)
        shard = jnp.concatenate([before, shard, after], axis=dim)
    return shard


def root_norm(values_in):
    return values_in * lax.rsqrt(jnp.mean(values_in * values_in, axis=-1, keepdims=True) + norm_eps)


def prepare(raw):
    return jax.nn.gelu(root_norm(raw.astype(jnp.float32)), approximate=False).astype(jnp.bfloat16)


def tap_sum(source, out_rows, tap_count, running, filter_rows):
    for lag_index in range(tap_count):
        running = running + jnp.dot(
            source[lag_index : lag_index + out_rows],
            filter_rows[lag_index],
            preferred_element_type=jnp.float32,
        )
    return running


def per_device(
    features,
    conv_weight,
    norm_gain,
    query_weight,
    keyval_weight,
    head_scale,
    output_weight,
    pair_weight,
    pair_input,
    flip_weight,
    pair_cotangent,
):
    fine_rows = features.shape[1]
    coarse_rows = fine_rows // 2
    in_channels = features.shape[2]
    model_dim = output_weight.shape[1]
    head_count = head_scale.shape[0]
    key_dim = query_weight.shape[1] // head_count
    pair_dim = flip_weight.shape[0]
    tap_count = conv_weight.shape[0]
    margin = tap_count // 2
    padded = padded_2(features, ((("seq", "mp"), 1),), margin)
    prepared = prepare(padded[0])
    starting = jnp.zeros((fine_rows, model_dim), jnp.float32)
    conv_sum = tap_sum(
        prepared,
        fine_rows,
        tap_count,
        starting,
        lax.all_gather(conv_weight, ("seq", "mp"), axis=1, tiled=True),
    )
    skipped = jnp.pad(features[0].astype(jnp.float32), ((0, 0), (0, model_dim - in_channels)))
    encoded = jnp.max((conv_sum + skipped).reshape(coarse_rows, 2, model_dim), axis=1).astype(
        jnp.bfloat16
    )
    widened = encoded.astype(jnp.float32)
    normed = (root_norm(widened) * norm_gain).astype(jnp.bfloat16)
    scale_row = jnp.repeat(head_scale, key_dim) / math.sqrt(key_dim)
    queries = (
        jnp.dot(normed, query_weight, preferred_element_type=jnp.float32) * scale_row
    ).astype(jnp.bfloat16)
    keyvals = jnp.dot(normed, keyval_weight, preferred_element_type=jnp.float32).astype(
        jnp.bfloat16
    )
    pooled = jnp.mean(
        widened.reshape(coarse_rows // PAIR_POOL, PAIR_POOL, model_dim), axis=1
    ).astype(jnp.bfloat16)
    pair_feats = jnp.dot(pooled, pair_weight, preferred_element_type=jnp.float32).astype(
        jnp.bfloat16
    )
    pair_q = pair_feats[:, :pair_dim]
    pair_k = pair_feats[:, pair_dim:]
    keys_all, pairk_all = (
        lax.all_gather(keyvals[None], ("seq", "mp"), axis=1, tiled=True),
        lax.all_gather(pair_k[None], ("seq", "mp"), axis=1, tiled=True),
    )
    summed = (
        pair_input[0].astype(jnp.float32)
        + pair_q[:, None, :].astype(jnp.float32) * pairk_all[0][None, :, :].astype(jnp.float32)
    ).astype(jnp.bfloat16)
    flipped = lax.all_to_all(summed[None], ("seq", "mp"), split_axis=2, concat_axis=1, tiled=True)[
        0
    ]
    turned = jnp.einsum("bac,cd->abd", flipped, flip_weight, preferred_element_type=jnp.float32)
    pair_out = (summed.astype(jnp.float32) + turned).astype(jnp.bfloat16)
    grad_term = jnp.einsum(
        "bac,abd->cd", flipped, pair_cotangent[0], preferred_element_type=jnp.float32
    )
    grad_flip = lax.psum(grad_term, ("dp", "seq", "mp"))
    key_rows = keys_all[0][:, :key_dim]
    value_rows = keys_all[0][:, key_dim:]
    query_rows = queries.reshape(coarse_rows * head_count, key_dim)
    scores = jnp.dot(query_rows, key_rows.T, preferred_element_type=jnp.float32)
    weights = jnp.exp(logit_cap * jnp.tanh(scores / logit_cap))
    totals = jnp.sum(weights, axis=-1, keepdims=True)
    mixed = (
        jnp.dot(weights.astype(jnp.bfloat16), value_rows, preferred_element_type=jnp.float32)
        / totals
    )
    heads_out = mixed.astype(jnp.bfloat16).reshape(coarse_rows, head_count * value_rows.shape[1])
    block_out = (
        widened + jnp.dot(heads_out, output_weight, preferred_element_type=jnp.float32)
    ).astype(jnp.bfloat16)
    return (block_out[None], pair_out[None], grad_flip)


def solution(mesh):
    placed = (
        P("dp", ("seq", "mp"), None),
        P(None, ("seq", "mp"), None),
        P(),
        P(),
        P(),
        P(),
        P(),
        P(),
        P("dp", ("seq", "mp"), None, None),
        P(),
        P("dp", ("seq", "mp"), None, None),
    )
    return jax.shard_map(
        per_device,
        mesh=mesh,
        in_specs=placed,
        out_specs=(P("dp", ("seq", "mp"), None), P("dp", ("seq", "mp"), None, None), P()),
        check_vma=False,
    )
```

profile of v0, /device:TPU:1, one launch (start us, length us, event | category | flops | bytes accessed | tf_op | source)
XLA Modules:
  0.0 959.2 jit_solution(9439417309653292819)
XLA Ops:
  7.2 2.7 copy.24
  12.0 10.3 %collective-permute-start = (bf16[1,2,1408]{2,1,0:T(2,128)(2,1)S(1)}, bf16[1,2,1408]{2,1,0:T(2,128)(2,1)S(1)}, u32[]{:S(2)}, u32[]{:S(2)}) collective-permute-start(bf16[1,2,1408]{2,1,0:T(2,128)(2,1)S(1)} %get-tuple-element.8), channel_id=1, source_target_pairs={{0,1},{1,2},{2,3},{3,4},{4,5},{5,6},{6,7},{7,8},{8,9},{9,10},{10,1... | collective-permute-start | bytes 16904 | tf_op jit(solution)/shard_map/ppermute | solution.py:19
  24.5 6.0 fusion.20
  30.5 426.3 %all-gather.5.cloned.1.call-done = bf16[5,1408,1536]{2,0,1:T(8,128)(2,1)} async-done(((bf16[5,44,1536]{2,0,1:T(8,128)(2,1)}), bf16[5,1408,1536]{2,0,1:T(8,128)(2,1)}) %all-gather.5.cloned.1.call-update) | async-done | bytes 21626896 | tf_op jit(solution)/shard_map/all_gather | solution.py:73
  456.8 92.6 %fusion.83 = (bf16[1,1408,1536]{2,0,1:T(2,128)(2,1)S(1)}, bf16[1,1408,1536]{2,0,1:T(2,128)(2,1)S(1)}, bf16[1,1408,1536]{2,0,1:T(2,128)(2,1)}, bf16[1,1408,1536]{2,0,1:T(2,128)(2,1)}, bf16[1,1408,1536]{2,0,1:T(2,128)(2,1)}) fusion(bf16[5,1408,1536]{2,0,1:T(8,128)(2,1)} %all-gather.5.cloned.1.call-done), kind=kLoop, calls=%fused_computation.101 | loop fusion | bytes 43253760 | tf_op jit(solution)/shard_map/slice | solution.py:37
  549.4 5.0 fusion.7
  554.5 4.9 fusion.9
  562.3 2.3 fusion.13
  564.6 2.9 reshape.58
  567.5 3.0 reduce_max.9
  570.7 2.3 convolution_convert_fusion
  574.6 105.2 %all-gather.1 = bf16[256,128]{1,0:T(8,128)(2,1)S(1)} all-gather(bf16[8,128]{1,0:T(8,128)(2,1)S(1)} %get-tuple-element.11), channel_id=3, replica_groups=mesh['dp'=8,'seq'=16,'mp'=2] {'seq','mp'}, dimensions={0}, use_global_device_ids=true | all-gather | bytes 67584 | tf_op jit(solution)/shard_map/all_gather | solution.py:98
  681.6 4.6 all-to-all-start
  688.3 1.8 reshape.59
  690.1 9.7 %all-to-all-done = bf16[1,8,256,128]{3,1,0,2:T(8,128)(2,1)} async-done(((bf16[1,8,256,128]{3,1,0,2:T(8,128)(2,1)}), bf16[1,8,256,128]{3,1,0,2:T(8,128)(2,1)}, u32[]{:S(2)}, u32[]{:S(2)}) %all-to-all-start) | async-done | bytes 524320 | tf_op jit(solution)/shard_map/all_to_all | solution.py:104
  699.8 2.2 convolution_bitcast_fusion.1
  702.0 2.3 fusion.51
  704.4 6.7 fusion
  711.1 5.9 fusion.63
  717.0 2.0 copy.30
  719.0 2.3 reshape.60
  721.3 4.0 fusion.15
  725.3 225.9 %all-reduce.3.cloned.1.call-done = f32[128,128]{1,0:T(8,128)} async-done(((f32[128,128]{1,0:T(8,128)}), f32[128,128]{1,0:T(8,128)}) %all-reduce.3.cloned.1.call-update) | async-done | bytes 65552 | tf_op jit(solution)/shard_map/psum | solution.py:112
  951.2 1.5 copy.69
  (47 shorter events, 12.8 us)
Async XLA Ops:
  7.2 679.8 %copy-start = (bf16[1536,1024]{1,0:T(8,128)(2,1)S(1)}, bf16[1536,1024]{1,0:T(8,128)(2,1)}, u32[]{:S(2)}) copy-start(bf16[1536,1024]{1,0:T(8,128)(2,1)} %param.14) | copy-start | bytes 9437188
  7.2 449.6 %all-gather.5.cloned.1.call-start = ((), (), s32[]{:S(2)}) async-start(), calls=%async_computation.1 | async-start | bytes 35684352 | tf_op jit(solution)/shard_map/all_gather | solution.py:73
  9.9 694.5 %all-gather.7.cloned.1.call-start = ((), (), s32[]{:S(2)}) async-start(), calls=%async_computation.3 | async-start | bytes 2703360 | tf_op jit(solution)/shard_map/all_gather | solution.py:97
  10.7 11.6 %collective-permute-start.1 = (bf16[1,2,1408]{2,1,0:T(2,128)(2,1)S(1)}, bf16[1,2,1408]{2,1,0:T(2,128)(2,1)S(1)}, u32[]{:S(2)}, u32[]{:S(2)}) collective-permute-start(bf16[1,2,1408]{2,1,0:T(2,128)(2,1)S(1)} %get-tuple-element.9), channel_id=1, source_target_pairs={{1,0},{2,1},{3,2},{4,3},{5,4},{6,5},{7,6},{8,7},{9,8},{10,9},{11,1... | collective-permute-start | bytes 16904 | tf_op jit(solution)/shard_map/ppermute | solution.py:20
  12.0 11.0 %collective-permute-start = (bf16[1,2,1408]{2,1,0:T(2,128)(2,1)S(1)}, bf16[1,2,1408]{2,1,0:T(2,128)(2,1)S(1)}, u32[]{:S(2)}, u32[]{:S(2)}) collective-permute-start(bf16[1,2,1408]{2,1,0:T(2,128)(2,1)S(1)} %get-tuple-element.8), channel_id=1, source_target_pairs={{0,1},{1,2},{2,3},{3,4},{4,5},{5,6},{6,7},{7,8},{8,9},{9,10},{10,1... | collective-permute-start | bytes 16904 | tf_op jit(solution)/shard_map/ppermute | solution.py:19
  456.8 92.6 %copy-start.4 = (bf16[260,1408]{1,0:T(8,128)(2,1)S(1)}, bf16[260,1408]{1,0:T(8,128)(2,1)}, u32[]{:S(2)}) copy-start(bf16[260,1408]{1,0:T(8,128)(2,1)} %fusion.20) | copy-start | bytes 2196484
  549.4 9.9 %slice-start = ((s8[8650752]{0:T(1024)(128)(4,1)}), s8[4194304]{0:T(1024)(128)(4,1)S(1)}, s32[]{:S(2)}) async-start(s8[8650752]{0:T(1024)(128)(4,1)} %bitcast.79), calls=%async_computation.4 | async-start | bytes 8388608
  549.4 9.9 %slice-start.1 = ((s8[8650752]{0:T(1024)(128)(4,1)}), s8[4194304]{0:T(1024)(128)(4,1)S(1)}, s32[]{:S(2)}) async-start(s8[8650752]{0:T(1024)(128)(4,1)} %bitcast.79), calls=%async_computation.5 | async-start | bytes 8388608
  554.4 4.9 slice-start.2
  560.8 1.4 copy-start.1
  564.6 6.1 copy-start.5
  573.0 106.8 %copy-start.2 = (bf16[1,8,256,128]{3,2,1,0:T(8,128)(2,1)S(1)}, bf16[1,8,256,128]{3,2,1,0:T(8,128)(2,1)}, u32[]{:S(2)}) copy-start(bf16[1,8,256,128]{3,2,1,0:T(8,128)(2,1)} %param.19) | copy-start | bytes 1572868
  679.8 0.6 copy-start.3
  681.6 18.2 %all-to-all-start = ((bf16[1,8,256,128]{3,1,0,2:T(8,128)(2,1)}), bf16[1,8,256,128]{3,1,0,2:T(8,128)(2,1)}, u32[]{:S(2)}, u32[]{:S(2)}) async-start(bf16[1,8,256,128]{3,1,0,2:T(8,128)(2,1)} %copy.31), calls=%async_computation | async-start | bytes 1048576 | tf_op jit(solution)/shard_map/all_to_all | solution.py:104
  686.2 264.9 %all-reduce.3.cloned.1.call-start = ((), (), s32[]{:S(2)}) async-start(), calls=%async_computation.2 | async-start | bytes 131072 | tf_op jit(solution)/shard_map/psum | solution.py:112
  704.4 6.7 copy-start.6
Sparse Core Ops, SparseCore 0:
  11.4 445.3 all-gather.4
  573.2 103.0 all-gather.6
  704.5 246.6 all-reduce.2
where the time goes:
time: 960 us; the launch traced here: 959 us
  waiting for transfers between devices  663 us (69%)
  local copies, waits for them, and re-layouts  108 us (11%)
  blocking collectives  105 us (11%)
  matrix products  41.2 us (4%)
  starting transfers between devices  16.3 us (2%)
  between operations  14 us (1%)
  other arithmetic  11.6 us (1%)
    all_gather x1, waiting for transfers between devices, per_device(): lax.all_gather(conv_weight, ('seq', 'mp'), axis=1, tiled=True)  426 us
    psum x1, waiting for transfers between devices, per_device(): grad_flip = lax.psum(grad_term, ('dp', 'seq', 'mp'))  226 us
    all_gather x1, blocking collectives, per_device(): lax.all_gather(pair_k[None], ('seq', 'mp'), axis=1, tiled=True)  105 us
    slice x1, local copies, waits for them, and re-layouts, tap_sum(): filter_rows[lag_index]  92.6 us
  transfers between devices with their start and end apart: 6, of which 4 were waited for; matrix products, arithmetic and copies ran while one was open for 4% of the time, Pallas kernels for 0%

commit v1 on v0

--- a/solution.py
+++ b/solution.py
@@ -109,7 +109,7 @@
     grad_term = jnp.einsum(
         "bac,abd->cd", flipped, pair_cotangent[0], preferred_element_type=jnp.float32
     )
-    grad_flip = lax.psum(grad_term, ("dp", "seq", "mp"))
+    grad_flip = lax.psum(lax.psum(grad_term, "dp"), ("seq", "mp"))
     key_rows = keys_all[0][:, :key_dim]
     value_rows = keys_all[0][:, key_dim:]
     query_rows = queries.reshape(coarse_rows * head_count, key_dim)

time: 960 us -> 1280 us (1.33); the launches traced: 959 us -> 1260 us
  waiting for transfers between devices: 663 us -> 972 us
    psum x1 -> x2, waiting for transfers between devices: 226 us -> 420 us  [per_device(): grad_flip = lax.psum(lax.psum(grad_term, 'dp'), ('seq', 'mp'))]
    all_gather x1, waiting for transfers between devices: 0.02 us -> 111 us  [per_device(): lax.all_gather(keyvals[None], ('seq', 'mp'), axis=1, tiled=True)]
  transfers between devices with their start and end apart: 6 -> 7, of which waited for: 4 -> 6; matrix products, arithmetic and copies ran while one was open for 4% -> 3% of each run, Pallas kernels for 0% -> 0%
where the time goes in v1:
time: 1280 us; the launch traced here: 1260 us
  waiting for transfers between devices  972 us (76%)
  local copies, waits for them, and re-layouts  108 us (8%)
  blocking collectives  96.4 us (8%)
  matrix products  41.2 us (3%)
  starting transfers between devices  16.5 us (1%)
  between operations  14 us (1%)
    all_gather x1, waiting for transfers between devices, per_device(): lax.all_gather(conv_weight, ('seq', 'mp'), axis=1, tiled=True)  426 us
    psum x2, waiting for transfers between devices, per_device(): grad_flip = lax.psum(lax.psum(grad_term, 'dp'), ('seq', 'mp'))  420 us
    all_gather x1, waiting for transfers between devices, per_device(): lax.all_gather(keyvals[None], ('seq', 'mp'), axis=1, tiled=True)  111 us
    all_gather x1, blocking collectives, per_device(): lax.all_gather(pair_k[None], ('seq', 'mp'), axis=1, tiled=True)  96.4 us
    slice x1, local copies, waits for them, and re-layouts, tap_sum(): filter_rows[lag_index]  92.6 us
  transfers between devices with their start and end apart: 7, of which 6 were waited for; matrix products, arithmetic and copies ran while one was open for 3% of the time, Pallas kernels for 0%

profile of v1, /device:TPU:1, one launch (start us, length us, event | category | flops | bytes accessed | tf_op | source)
XLA Modules:
  0.0 1259.9 jit_solution(4507708547094996088)
XLA Ops:
  7.2 2.7 copy.24
  12.0 10.3 collective-permute-start
  24.5 6.0 fusion.20
  30.4 426.4 %all-gather.5.cloned.1.call-done = bf16[5,1408,1536]{2,0,1:T(8,128)(2,1)} async-done(((bf16[5,44,1536]{2,0,1:T(8,128)(2,1)}), bf16[5,1408,1536]{2,0,1:T(8,128)(2,1)}) %all-gather.5.cloned.1.call-update) | async-done | bytes 21626896 | tf_op jit(solution)/shard_map/all_gather | solution.py:73
  456.8 92.6 %fusion.83 = (bf16[1,1408,1536]{2,0,1:T(2,128)(2,1)S(1)}, bf16[1,1408,1536]{2,0,1:T(2,128)(2,1)S(1)}, bf16[1,1408,1536]{2,0,1:T(2,128)(2,1)}, bf16[1,1408,1536]{2,0,1:T(2,128)(2,1)}, bf16[1,1408,1536]{2,0,1:T(2,128)(2,1)}) fusion(bf16[5,1408,1536]{2,0,1:T(8,128)(2,1)} %all-gather.5.cloned.1.call-done), kind=kLoop, calls=%fused_computation.101 | loop fusion | bytes 43253760 | tf_op jit(solution)/shard_map/slice | solution.py:37
  549.4 5.0 fusion.7
  554.5 4.9 fusion.9
  562.3 2.3 fusion.13
  564.6 2.8 reshape.58
  567.5 3.0 reduce_max.9
  572.0 96.4 %all-gather.1 = bf16[256,128]{1,0:T(8,128)(2,1)S(1)} all-gather(bf16[8,128]{1,0:T(8,128)(2,1)S(1)} %get-tuple-element.11), channel_id=3, replica_groups=mesh['dp'=8,'seq'=16,'mp'=2] {'seq','mp'}, dimensions={0}, use_global_device_ids=true | all-gather | bytes 67584 | tf_op jit(solution)/shard_map/all_gather | solution.py:98
  670.2 4.8 all-to-all-start
  675.2 13.4 %all-to-all-done = bf16[1,8,256,128]{3,1,0,2:T(8,128)(2,1)} async-done(((bf16[1,8,256,128]{3,1,0,2:T(8,128)(2,1)}), bf16[1,8,256,128]{3,1,0,2:T(8,128)(2,1)}, u32[]{:S(2)}, u32[]{:S(2)}) %all-to-all-start) | async-done | bytes 524320 | tf_op jit(solution)/shard_map/all_to_all | solution.py:104
  688.6 2.2 convolution_bitcast_fusion.1
  690.9 2.3 convolution_convert_fusion
  697.1 2.3 fusion.51
  699.4 66.9 %all-reduce.4.cloned.1.call-done = f32[128,128]{1,0:T(8,128)} async-done(((f32[128,128]{1,0:T(8,128)}), f32[128,128]{1,0:T(8,128)}) %all-reduce.4.cloned.1.call-update) | async-done | bytes 65552 | tf_op jit(solution)/shard_map/psum | solution.py:112
  766.3 111.3 %all-gather.7.cloned.1.call-done = bf16[4096,320]{0,1:T(8,128)(2,1)} async-done(((bf16[128,320]{0,1:T(8,128)(2,1)}), bf16[4096,320]{0,1:T(8,128)(2,1)}) %all-gather.7.cloned.1.call-update) | async-done | bytes 2621456 | tf_op jit(solution)/shard_map/all_gather | solution.py:97
  877.7 6.6 fusion
  884.3 5.9 fusion.63
  890.3 2.0 copy.30
  892.3 2.3 reshape.60
  894.5 4.0 fusion.15
  898.6 353.4 %all-reduce.6.cloned.1.call-done = f32[128,128]{1,0:T(8,128)} async-done(((f32[128,128]{1,0:T(8,128)}), f32[128,128]{1,0:T(8,128)}) %all-reduce.6.cloned.1.call-update) | async-done | bytes 65552 | tf_op jit(solution)/shard_map/psum | solution.py:112
  (50 shorter events, 16.1 us)
Async XLA Ops:
  7.2 686.8 %copy-start = (bf16[1536,1024]{1,0:T(8,128)(2,1)S(1)}, bf16[1536,1024]{1,0:T(8,128)(2,1)}, u32[]{:S(2)}) copy-start(bf16[1536,1024]{1,0:T(8,128)(2,1)} %param.14) | copy-start | bytes 9437188
  7.2 449.6 %all-gather.5.cloned.1.call-start = ((), (), s32[]{:S(2)}) async-start(), calls=%async_computation.1 | async-start | bytes 35684352 | tf_op jit(solution)/shard_map/all_gather | solution.py:73
  10.7 11.6 collective-permute-start.1
  12.0 11.0 collective-permute-start
  456.8 92.6 %copy-start.4 = (bf16[260,1408]{1,0:T(8,128)(2,1)S(1)}, bf16[260,1408]{1,0:T(8,128)(2,1)}, u32[]{:S(2)}) copy-start(bf16[260,1408]{1,0:T(8,128)(2,1)} %fusion.20) | copy-start | bytes 2196484
  549.4 9.9 slice-start
  549.4 9.9 slice-start.1
  554.4 4.9 slice-start.2
  560.8 1.4 copy-start.1
  570.5 98.0 %copy-start.2 = (bf16[1,8,256,128]{3,2,1,0:T(8,128)(2,1)S(1)}, bf16[1,8,256,128]{3,2,1,0:T(8,128)(2,1)}, u32[]{:S(2)}) copy-start(bf16[1,8,256,128]{3,2,1,0:T(8,128)(2,1)} %param.19) | copy-start | bytes 1572868
  668.4 0.6 copy-start.3
  670.2 20.6 %copy-start.5 = (f32[1536]{0:T(1024)S(1)}, f32[1536]{0:T(1024)}, u32[]{:S(2)}) copy-start(f32[1536]{0:T(1024)} %param.13) | copy-start | bytes 18436
  670.2 18.4 %all-to-all-start = ((bf16[1,8,256,128]{3,1,0,2:T(8,128)(2,1)}), bf16[1,8,256,128]{3,1,0,2:T(8,128)(2,1)}, u32[]{:S(2)}, u32[]{:S(2)}) async-start(bf16[1,8,256,128]{3,1,0,2:T(8,128)(2,1)} %copy.31), calls=%async_computation | async-start | bytes 1048576 | tf_op jit(solution)/shard_map/all_to_all | solution.py:104
  675.0 91.3 %all-reduce.4.cloned.1.call-start = ((), (), s32[]{:S(2)}) async-start(), calls=%async_computation.2 | async-start | bytes 131072 | tf_op jit(solution)/shard_map/psum | solution.py:112
  690.8 186.9 %all-gather.7.cloned.1.call-start = ((), (), s32[]{:S(2)}) async-start(), calls=%async_computation.4 | async-start | bytes 2703360 | tf_op jit(solution)/shard_map/all_gather | solution.py:97
  693.2 558.7 %all-reduce.6.cloned.1.call-start = ((), (), s32[]{:S(2)}) async-start(), calls=%async_computation.3 | async-start | bytes 131072 | tf_op jit(solution)/shard_map/psum | solution.py:112
  877.7 6.7 copy-start.6
Sparse Core Ops, SparseCore 0:
  11.4 445.3 all-gather.4
  690.9 75.3 all-reduce.3
  770.0 107.6 all-gather.6
  880.3 371.5 all-reduce.5
